TPU v7x, 32 devices: a whole 2x2x4 slice. The times are simulated.
32 devices in a mesh: dom: 8 (over z, x), grp: 4 (over y, core).
Axes of the slice: x: 2, y: 2, z: 4, core: 2. Of those that a mesh axis runs over, the one named last changes fastest.
Arguments:
- features: bfloat16 [32768, 512], P(('dom', 'grp')), may hold values from -6 to 6
- tile_src: int32 [256, 8], P(('dom', 'grp')), may hold values from 0 to 8
- tile_val: bfloat16 [256, 8, 128, 128], P(('dom', 'grp')), may hold values from -0.1875 to 0.1875
- send_sel: int32 [32, 8], P(('dom', 'grp')), may hold values from 0 to 63
- stale_features: bfloat16 [4096, 512], P(('dom', 'grp')), may hold values from -5 to 5
- stale_grads: bfloat16 [4096, 512], P(('dom', 'grp')), may hold values from -6 to 6
- out_grad: bfloat16 [32768, 512], P(('dom', 'grp')), may hold values from -6 to 6
- master: float32 [2, 512, 512], P(None, ('dom', 'grp')), may hold values from -0.25 to 0.25
- moment_first: float32 [2, 512, 512], P(None, ('dom', 'grp')), may hold values from -0.0234375 to 0.0234375
- moment_second: float32 [2, 512, 512], P(None, ('dom', 'grp')), may hold values from 6.1035155e-07 to 1.5258789e-05
Outputs:
- layer_out: bfloat16 [32768, 512], P(('dom', 'grp'))
- fresh_features: bfloat16 [4096, 512], P(('dom', 'grp'))
- fresh_grads: bfloat16 [4096, 512], P(('dom', 'grp'))
- master_next: float32 [2, 512, 512], P(None, ('dom', 'grp'))
- weights_next: bfloat16 [2, 512, 512], replicated
Inputs may be any that keep to these rules, and one draw needn't show every extreme that they name: `tile_src`: A value below 8 names a local row block; 8 + b names boundary block b.
All inputs are finite; a program needn't handle non-finite values.
Results may differ from a plain program's by a relative error of at most 0.005.
The roundings to bfloat16 on the way count: a program that leaves them out, or rounds other values in their place, can miss the bound.
Values may be sent and summed in bfloat16 or wider, within the bound.
No kernel may reach another device: no remote copies, remote signals or barrier semaphores. Data moves between devices by JAX's collectives and lax.ppermute only.
A program may use at most 128 MiB of HBM per device.

v0:
```python
import jax
import jax.numpy as jnp
from jax import lax
from jax.sharding import PartitionSpec as P

STEP = 10
decay_first = 0.9
decay_second = 0.95
learn_rate = 0.01
epsilon = 1e-08


def aggregate(local_rows, rim_rows, tile_val, tile_src):
    edge = tile_val.shape[2]
    lookup = jnp.concatenate([local_rows, rim_rows], 0).reshape(-1, edge, local_rows.shape[1])
    picked = lookup[tile_src]
    total = jnp.einsum("rtij,rtjf->rif", tile_val, picked, preferred_element_type=jnp.float32)
    return total.reshape(-1, local_rows.shape[1])


def per_device(
    features,
    tile_src,
    tile_val,
    send_sel,
    stale_features,
    stale_grads,
    out_grad,
    master,
    moment_first,
    moment_second,
):
    peers = lax.axis_size("dom")
    devices = peers * lax.axis_size("grp")
    total_nodes = features.shape[0] * devices
    feature_width = features.shape[1]
    blocks, tiles_row, edge = (tile_val.shape[0], tile_val.shape[1], tile_val.shape[2])
    piece_rows = stale_features.shape[0] // peers
    local_count = features.shape[0]
    selects = send_sel[0]
    weights = lax.all_gather(master.astype(jnp.bfloat16), ("dom", "grp"), axis=1, tiled=True)
    w_first, w_second = (weights[0], weights[1])

    def outgoing(node_rows):
        pieces = node_rows.reshape(-1, piece_rows, feature_width)
        return jnp.take(pieces, selects, axis=0)

    raw_rim = lax.all_to_all(
        outgoing(features), "dom", split_axis=0, concat_axis=0, tiled=True
    ).reshape(-1, feature_width)
    p_first = aggregate(features, raw_rim, tile_val, tile_src).astype(jnp.bfloat16)
    z_first = jnp.dot(p_first, w_first, preferred_element_type=jnp.float32)
    h_first = jax.nn.silu(z_first).astype(jnp.bfloat16)
    p_second = aggregate(h_first, stale_features, tile_val, tile_src).astype(jnp.bfloat16)
    layer_out = jnp.dot(p_second, w_second, preferred_element_type=jnp.float32).astype(jnp.bfloat16)
    upstream = lax.dot_general(
        out_grad, w_second, (((1,), (1,)), ((), ())), preferred_element_type=jnp.float32
    ).astype(jnp.bfloat16)
    g_second = lax.dot_general(
        p_second, out_grad, (((0,), (0,)), ((), ())), preferred_element_type=jnp.float32
    )
    up_blocks = upstream.reshape(blocks, edge, feature_width)
    slots = blocks + stale_features.shape[0] // edge
    spreads = jnp.zeros((slots, edge, feature_width), jnp.float32)
    for column in range(tiles_row):
        product = jnp.einsum(
            "rij,rif->rjf", tile_val[:, column], up_blocks, preferred_element_type=jnp.float32
        )
        spreads = spreads.at[tile_src[:, column]].add(product)
    spreads = spreads.reshape(-1, feature_width)
    local_part = spreads[:local_count]
    rim_part = spreads[local_count:].astype(jnp.bfloat16).reshape(peers, piece_rows, feature_width)
    fresh_features = lax.all_to_all(
        outgoing(h_first), "dom", split_axis=0, concat_axis=0, tiled=True
    ).reshape(-1, feature_width)
    fresh_grads = lax.all_to_all(rim_part, "dom", split_axis=0, concat_axis=0, tiled=True).reshape(
        -1, feature_width
    )
    piece_count = local_count // piece_rows
    placing = (selects[:, None] == jnp.arange(piece_count, dtype=jnp.int32)[None, :]).astype(
        jnp.float32
    )
    stale_slots = stale_grads.reshape(peers, piece_rows, feature_width).astype(jnp.float32)
    placed = jnp.einsum("pq,prf->qrf", placing, stale_slots, precision=lax.Precision.HIGHEST)
    d_first = local_part + placed.reshape(-1, feature_width)
    sigma = jax.nn.sigmoid(z_first)
    dz = (d_first * sigma * (1.0 + z_first * (1.0 - sigma))).astype(jnp.bfloat16)
    g_first = lax.dot_general(
        p_first, dz, (((0,), (0,)), ((), ())), preferred_element_type=jnp.float32
    )
    grads = jnp.stack([g_first, g_second])
    partial_sum = lax.psum_scatter(grads, "dom", scatter_dimension=1, tiled=True)
    shard = (
        lax.psum_scatter(
            partial_sum.astype(jnp.bfloat16), "grp", scatter_dimension=1, tiled=True
        ).astype(jnp.float32)
        / total_nodes
    )
    moment_new = decay_first * moment_first + (1.0 - decay_first) * shard
    second_new = decay_second * moment_second + (1.0 - decay_second) * shard * shard
    update = (
        moment_new
        / (1.0 - decay_first**STEP)
        / (jnp.sqrt(second_new / (1.0 - decay_second**STEP)) + epsilon)
    )
    master_next = master - learn_rate * update
    rounded = master_next.astype(jnp.bfloat16)
    group_part = lax.all_gather(rounded, "grp", axis=1, tiled=True)
    weights_next = lax.all_gather(group_part, "dom", axis=1, tiled=True)
    return (layer_out, fresh_features, fresh_grads, master_next, weights_next)


def solution(mesh):
    placed = (
        P(("dom", "grp"), None),
        P(("dom", "grp"), None),
        P(("dom", "grp"), None, None, None),
        P(("dom", "grp"), None),
        P(("dom", "grp"), None),
        P(("dom", "grp"), None),
        P(("dom", "grp"), None),
        P(None, ("dom", "grp"), None),
        P(None, ("dom", "grp"), None),
        P(None, ("dom", "grp"), None),
    )
    return jax.shard_map(
        per_device,
        mesh=mesh,
        in_specs=placed,
        out_specs=(
            P(("dom", "grp"), None),
            P(("dom", "grp"), None),
            P(("dom", "grp"), None),
            P(None, ("dom", "grp"), None),
            P(),
        ),
        check_vma=False,
    )
```

profile of v0, /device:TPU:0, one launch (start us, length us, event | category | flops | bytes accessed | tf_op | source)
XLA Modules:
  0.0 301.4 jit_solution(9451893326494753494)
XLA Ops:
  12.7 7.3 %all-to-all-start = ((bf16[8,16,512]{2,1,0:T(8,128)(2,1)}), bf16[8,16,512]{2,1,0:T(8,128)(2,1)S(1)}, u32[]{:S(2)}, u32[]{:S(2)}) async-start(bf16[8,16,512]{2,1,0:T(8,128)(2,1)} %broadcast_select_fusion.1), calls=%async_computation | async-start | bytes 262144 | tf_op jit(solution)/shard_map/all_to_all | solution.py:48
  21.6 2.6 copy.40
  24.5 2.8 all-to-all-done
  28.6 5.7 %gather_fusion = bf16[64,128,512]{2,1,0:T(8,128)(2,1)} fusion(bf16[9,128,512]{2,1,0:T(8,128)(2,1)S(1)} %bitcast.129, s32[1024]{0:T(1024)S(1)} %pad_clamp_fusion), kind=kCustom, calls=%fused_computation.2 | custom fusion | bytes 16777472 | tf_op jit(solution)/shard_map/gather | solution.py:16
  34.3 6.3 %bitcast_convert_fusion.1 = bf16[8,512,128]{1,2,0:T(8,128)(2,1)} fusion(bf16[8,8,128,128]{3,2,1,0:T(8,128)(2,1)} %param.14, bf16[8,8,128,512]{3,2,1,0:T(8,128)(2,1)} %bitcast.140), kind=kOutput, calls=%fused_computation.18 | convolution fusion | flops 1074266112 | bytes 11534336 | tf_op jit(solution)/shard_map/rtij,rtjf->rif/dot_general | solution.py:17
  40.6 27.3 %all-gather.3.cloned.1.call-done = bf16[2,512,512]{2,1,0:T(8,128)(2,1)} async-done(((bf16[2,16,512]{2,1,0:T(8,128)(2,1)}), bf16[2,512,512]{2,1,0:T(8,128)(2,1)}) %all-gather.3.cloned.1.call-update) | async-done | bytes 1048592 | tf_op jit(solution)/shard_map/all_gather | solution.py:41
  77.0 1.9 convolution_bitcast_fusion.3
  84.4 3.1 %copy.17 = f32[8,128,512]{2,1,0:T(8,128)} copy(f32[8,128,512]{1,2,0:T(8,128)} %convolution_bitcast_fusion.7) | data formatting | bytes 4194304 | tf_op jit(solution)/shard_map/rij,rif->rjf/dot_general | solution.py:66
  89.3 3.0 %copy.23 = f32[8,128,512]{2,1,0:T(8,128)} copy(f32[8,128,512]{1,2,0:T(8,128)} %convolution_bitcast_fusion.5) | data formatting | bytes 4194304 | tf_op jit(solution)/shard_map/rij,rif->rjf/dot_general | solution.py:66
  92.4 1.9 copy.26
  94.3 3.0 %copy.29 = f32[8,128,512]{2,1,0:T(8,128)} copy(f32[8,128,512]{1,2,0:T(8,128)} %convolution_bitcast_fusion.3) | data formatting | bytes 4194304 | tf_op jit(solution)/shard_map/rij,rif->rjf/dot_general | solution.py:66
  99.2 3.1 %copy.35 = f32[8,128,512]{2,1,0:T(8,128)} copy(f32[8,128,512]{1,2,0:T(8,128)} %convolution_bitcast_fusion.1) | data formatting | bytes 4194304 | tf_op jit(solution)/shard_map/rij,rif->rjf/dot_general | solution.py:66
  104.3 3.4 %scatter_fusion = f32[9,128,512]{2,1,0:T(8,128)S(1)} fusion(f32[9,128,512]{2,1,0:T(8,128)S(1)} %broadcast_in_dim.14, s32[8]{0:T(128)S(1)} %get-tuple-element.10, f32[8,128,512]{2,1,0:T(8,128)} %copy.17), kind=kCustom, calls=%fused_computation.4 | custom fusion | flops 524288 | bytes 6291488 | tf_op jit(solution)/shard_map/scatter-add | solution.py:69
  107.7 3.3 %scatter_fusion.1 = f32[9,128,512]{2,1,0:T(8,128)S(1)} fusion(f32[9,128,512]{2,1,0:T(8,128)S(1)} %scatter_fusion, s32[8]{0:T(128)S(1)} %get-tuple-element.9, f32[8,128,512]{2,1,0:T(8,128)} %copy.20), kind=kCustom, calls=%fused_computation.5 | custom fusion | flops 524288 | bytes 6291488 | tf_op jit(solution)/shard_map/scatter-add | solution.py:69
  111.1 3.6 %scatter_fusion.2 = f32[9,128,512]{2,1,0:T(8,128)S(1)} fusion(f32[9,128,512]{2,1,0:T(8,128)S(1)} %scatter_fusion.1, s32[8]{0:T(128)S(1)} %get-tuple-element.8, f32[8,128,512]{2,1,0:T(8,128)} %copy.23), kind=kCustom, calls=%fused_computation.6 | custom fusion | flops 524288 | bytes 6291488 | tf_op jit(solution)/shard_map/scatter-add | solution.py:69
  114.6 3.4 %scatter_fusion.3 = f32[9,128,512]{2,1,0:T(8,128)S(1)} fusion(f32[9,128,512]{2,1,0:T(8,128)S(1)} %scatter_fusion.2, s32[8]{0:T(128)S(1)} %get-tuple-element.7, f32[8,128,512]{2,1,0:T(8,128)} %copy.26), kind=kCustom, calls=%fused_computation.7 | custom fusion | flops 524288 | bytes 6291488 | tf_op jit(solution)/shard_map/scatter-add | solution.py:69
  118.0 3.4 %scatter_fusion.4 = f32[9,128,512]{2,1,0:T(8,128)S(1)} fusion(f32[9,128,512]{2,1,0:T(8,128)S(1)} %scatter_fusion.3, s32[8]{0:T(128)S(1)} %get-tuple-element.11, f32[8,128,512]{2,1,0:T(8,128)} %copy.29), kind=kCustom, calls=%fused_computation.8 | custom fusion | flops 524288 | bytes 6291488 | tf_op jit(solution)/shard_map/scatter-add | solution.py:69
  121.4 3.4 %scatter_fusion.5 = f32[9,128,512]{2,1,0:T(8,128)S(1)} fusion(f32[9,128,512]{2,1,0:T(8,128)S(1)} %scatter_fusion.4, s32[8]{0:T(128)S(1)} %get-tuple-element.12, f32[8,128,512]{2,1,0:T(8,128)} %copy.32), kind=kCustom, calls=%fused_computation.9 | custom fusion | flops 524288 | bytes 6291488 | tf_op jit(solution)/shard_map/scatter-add | solution.py:69
  124.7 3.4 %scatter_fusion.6 = f32[9,128,512]{2,1,0:T(8,128)S(1)} fusion(f32[9,128,512]{2,1,0:T(8,128)S(1)} %scatter_fusion.5, s32[8]{0:T(128)S(1)} %get-tuple-element.13, f32[8,128,512]{2,1,0:T(8,128)} %copy.35), kind=kCustom, calls=%fused_computation.10 | custom fusion | flops 524288 | bytes 6291488 | tf_op jit(solution)/shard_map/scatter-add | solution.py:69
  128.1 3.4 %scatter_fusion.7 = f32[9,128,512]{2,1,0:T(8,128)S(1)} fusion(f32[9,128,512]{2,1,0:T(8,128)S(1)} %scatter_fusion.6, s32[8]{0:T(128)S(1)} %get-tuple-element.6, f32[8,128,512]{2,1,0:T(8,128)} %copy.38), kind=kCustom, calls=%fused_computation.11 | custom fusion | flops 524288 | bytes 6291488 | tf_op jit(solution)/shard_map/scatter-add | solution.py:69
  138.0 6.8 %gather_fusion.1 = bf16[64,128,512]{2,1,0:T(8,128)(2,1)} fusion(bf16[9,128,512]{2,1,0:T(8,128)(2,1)} %bitcast.130, s32[1024]{0:T(1024)S(1)} %pad_clamp_fusion), kind=kCustom, calls=%fused_computation.3 | custom fusion | bytes 16777472 | tf_op jit(solution)/shard_map/gather | solution.py:16
  144.8 5.3 %bitcast_convert_fusion = bf16[8,512,128]{1,2,0:T(8,128)(2,1)S(1)} fusion(bf16[8,8,128,128]{3,2,1,0:T(8,128)(2,1)} %param.14, bf16[8,8,128,512]{3,2,1,0:T(8,128)(2,1)} %bitcast.139), kind=kOutput, calls=%fused_computation.17 | convolution fusion | flops 1074266112 | bytes 11534336 | tf_op jit(solution)/shard_map/rtij,rtjf->rif/dot_general | solution.py:17
  153.3 67.3 %reduce-scatter.3.cloned.1.call-done = f32[2,64,512]{2,1,0:T(8,128)} async-done(((f32[2,512,512]{2,1,0:T(8,128)}), f32[2,64,512]{2,1,0:T(8,128)}) %reduce-scatter.3.cloned.1.call-update) | async-done | bytes 262160 | tf_op jit(solution)/shard_map/reduce_scatter | solution.py:92
  222.3 20.0 %reduce-scatter.5.cloned.1.call-done = bf16[2,16,512]{2,1,0:T(8,128)(2,1)} async-done(((bf16[2,64,512]{2,1,0:T(8,128)(2,1)}), bf16[2,16,512]{2,1,0:T(8,128)(2,1)}) %reduce-scatter.5.cloned.1.call-update) | async-done | bytes 32784 | tf_op jit(solution)/shard_map/reduce_scatter | solution.py:94
  243.9 5.8 %all_gather.10 = bf16[2,64,512]{2,1,0:T(8,128)(2,1)} all-gather(bf16[2,16,512]{2,1,0:T(8,128)(2,1)S(1)} %get-tuple-element.14), channel_id=1, replica_groups=mesh['dom'=8,'grp'=4] {'grp'}, dimensions={1}, use_global_device_ids=true | all-gather | bytes 163840 | tf_op jit(solution)/shard_map/all_gather | solution.py:108
  252.3 5.5 %all-to-all-start.1 = ((bf16[8,16,512]{2,1,0:T(8,128)(2,1)}), bf16[8,16,512]{2,1,0:T(8,128)(2,1)S(1)}, u32[]{:S(2)}, u32[]{:S(2)}) async-start(bf16[8,16,512]{2,1,0:T(8,128)(2,1)} %broadcast_select_fusion), calls=%async_computation.1 | async-start | bytes 262144 | tf_op jit(solution)/shard_map/all_to_all | solution.py:73
  258.5 8.6 %all-to-all-done.1 = bf16[8,16,512]{2,1,0:T(8,128)(2,1)S(1)} async-done(((bf16[8,16,512]{2,1,0:T(8,128)(2,1)}), bf16[8,16,512]{2,1,0:T(8,128)(2,1)S(1)}, u32[]{:S(2)}, u32[]{:S(2)}) %all-to-all-start.1) | async-done | bytes 131104 | tf_op jit(solution)/shard_map/all_to_all | solution.py:73
  267.1 3.4 %all-to-all-start.2 = ((bf16[8,16,512]{2,1,0:T(8,128)(2,1)}), bf16[8,16,512]{2,1,0:T(8,128)(2,1)S(1)}, u32[]{:S(2)}, u32[]{:S(2)}) async-start(bf16[8,16,512]{2,1,0:T(8,128)(2,1)} %bitcast.150), calls=%async_computation.2 | async-start | bytes 262144 | tf_op jit(solution)/shard_map/all_to_all | solution.py:76
  270.5 3.0 %convolution_convert_fusion.1 = bf16[1024,512]{1,0:T(8,128)(2,1)} fusion(bf16[1024,512]{1,0:T(8,128)(2,1)} %bitcast.144, bf16[2,512,512]{2,1,0:T(8,128)(2,1)} %all-gather.3.cloned.1.call-done), kind=kOutput, calls=%fused_computation.30 | convolution fusion | flops 537395200 | bytes 2621440 | tf_op jit(solution)/shard_map/dot_general | solution.py:55
  273.5 4.2 %all-to-all-done.2 = bf16[8,16,512]{2,1,0:T(8,128)(2,1)S(1)} async-done(((bf16[8,16,512]{2,1,0:T(8,128)(2,1)}), bf16[8,16,512]{2,1,0:T(8,128)(2,1)S(1)}, u32[]{:S(2)}, u32[]{:S(2)}) %all-to-all-start.2) | async-done | bytes 131104 | tf_op jit(solution)/shard_map/all_to_all | solution.py:76
  277.8 13.6 %all-gather.5.cloned.1.call-done = bf16[2,512,512]{2,1,0:T(8,128)(2,1)} async-done(((bf16[2,64,512]{2,1,0:T(8,128)(2,1)}), bf16[2,512,512]{2,1,0:T(8,128)(2,1)}) %all-gather.5.cloned.1.call-update) | async-done | bytes 1048592 | tf_op jit(solution)/shard_map/all_gather | solution.py:109
  292.7 2.3 copy.74
  (77 shorter events, 46.5 us)
Async XLA Ops:
  7.2 60.7 %copy-start = (bf16[1024,512]{1,0:T(8,128)(2,1)S(1)}, bf16[1024,512]{1,0:T(8,128)(2,1)}, u32[]{:S(2)}) copy-start(bf16[1024,512]{1,0:T(8,128)(2,1)} %param.18) | copy-start | bytes 3145732
  7.2 14.3 %copy-start.11 = (s32[8,8]{1,0:T(8,128)S(1)}, s32[8,8]{1,0:T(8,128)}, u32[]{:S(2)}) copy-start(s32[8,8]{1,0:T(8,128)} %param.13) | copy-start | bytes 772
  7.2 60.7 %all-gather.3.cloned.1.call-start = ((), (), s32[]{:S(2)}) async-start(), calls=%async_computation.5 | async-start | bytes 1081344 | tf_op jit(solution)/shard_map/all_gather | solution.py:41
  12.7 14.6 %all-to-all-start = ((bf16[8,16,512]{2,1,0:T(8,128)(2,1)}), bf16[8,16,512]{2,1,0:T(8,128)(2,1)S(1)}, u32[]{:S(2)}, u32[]{:S(2)}) async-start(bf16[8,16,512]{2,1,0:T(8,128)(2,1)} %broadcast_select_fusion.1), calls=%async_computation | async-start | bytes 262144 | tf_op jit(solution)/shard_map/all_to_all | solution.py:48
  19.9 200.7 %reduce-scatter.3.cloned.1.call-start = ((), (), s32[]{:S(2)}) async-start(), calls=%async_computation.6 | async-start | bytes 2359296 | tf_op jit(solution)/shard_map/reduce_scatter | solution.py:92
  40.6 29.1 %copy-start.1 = (bf16[8,8,128,128]{3,2,1,0:T(8,128)(2,1)S(1)}, bf16[8,8,128,128]{3,2,1,0:T(8,128)(2,1)}, u32[]{:S(2)}) copy-start(bf16[8,8,128,128]{3,2,1,0:T(8,128)(2,1)} %param.14) | copy-start | bytes 6291460
  84.4 3.1 %copy-start.5 = (f32[8,128,512]{1,2,0:T(8,128)S(1)}, f32[8,128,512]{1,2,0:T(8,128)}, u32[]{:S(2)}) copy-start(f32[8,128,512]{1,2,0:T(8,128)} %convolution_bitcast_fusion.6) | copy-start | bytes 6291460
  89.3 3.0 %copy-start.4 = (f32[8,128,512]{1,2,0:T(8,128)S(1)}, f32[8,128,512]{1,2,0:T(8,128)}, u32[]{:S(2)}) copy-start(f32[8,128,512]{1,2,0:T(8,128)} %convolution_bitcast_fusion.4) | copy-start | bytes 6291460
  94.3 3.0 %copy-start.3 = (f32[8,128,512]{1,2,0:T(8,128)S(1)}, f32[8,128,512]{1,2,0:T(8,128)}, u32[]{:S(2)}) copy-start(f32[8,128,512]{1,2,0:T(8,128)} %convolution_bitcast_fusion.2) | copy-start | bytes 6291460
  99.1 3.1 %copy-start.2 = (f32[8,128,512]{1,2,0:T(8,128)S(1)}, f32[8,128,512]{1,2,0:T(8,128)}, u32[]{:S(2)}) copy-start(f32[8,128,512]{1,2,0:T(8,128)} %convolution_bitcast_fusion) | copy-start | bytes 6291460
  131.5 1.6 copy-start.6
  131.5 1.8 copy-start.10
  131.5 2.2 copy-start.15
  135.1 1.7 copy-start.7
  135.1 1.7 copy-start.13
  150.1 1.0 copy-start.9
  150.1 1.6 copy-start.8
  153.2 89.1 %copy-start.12 = (f32[2,16,512]{2,1,0:T(8,128)S(1)}, f32[2,16,512]{2,1,0:T(8,128)}, u32[]{:S(2)}) copy-start(f32[2,16,512]{2,1,0:T(8,128)} %param.19) | copy-start | bytes 196612
  153.2 89.1 %copy-start.14 = (f32[2,16,512]{2,1,0:T(8,128)S(1)}, f32[2,16,512]{2,1,0:T(8,128)}, u32[]{:S(2)}) copy-start(f32[2,16,512]{2,1,0:T(8,128)} %param.21) | copy-start | bytes 196612
  153.3 89.1 %reduce-scatter.5.cloned.1.call-start = ((), (), s32[]{:S(2)}) async-start(), calls=%async_computation.7 | async-start | bytes 163840 | tf_op jit(solution)/shard_map/reduce_scatter | solution.py:94
  222.3 69.1 %all-gather.5.cloned.1.call-start = ((), (), s32[]{:S(2)}) async-start(), calls=%async_computation.8 | async-start | bytes 1179648 | tf_op jit(solution)/shard_map/all_gather | solution.py:109
  252.3 14.8 %all-to-all-start.1 = ((bf16[8,16,512]{2,1,0:T(8,128)(2,1)}), bf16[8,16,512]{2,1,0:T(8,128)(2,1)S(1)}, u32[]{:S(2)}, u32[]{:S(2)}) async-start(bf16[8,16,512]{2,1,0:T(8,128)(2,1)} %broadcast_select_fusion), calls=%async_computation.1 | async-start | bytes 262144 | tf_op jit(solution)/shard_map/all_to_all | solution.py:73
  267.1 10.7 %all-to-all-start.2 = ((bf16[8,16,512]{2,1,0:T(8,128)(2,1)}), bf16[8,16,512]{2,1,0:T(8,128)(2,1)S(1)}, u32[]{:S(2)}, u32[]{:S(2)}) async-start(bf16[8,16,512]{2,1,0:T(8,128)(2,1)} %bitcast.150), calls=%async_computation.2 | async-start | bytes 262144 | tf_op jit(solution)/shard_map/all_to_all | solution.py:76
Sparse Core Ops, SparseCore 0:
  11.5 56.3 all-gather.2
  153.4 67.1 reduce-scatter.2
  223.6 18.6 reduce-scatter.4
  249.9 41.4 all-gather.4
where the time goes:
time: 303 us; the launch traced here: 301 us
  waiting for transfers between devices  144 us (48%)
  local copies, waits for them, and re-layouts  45.9 us (15%)
  other arithmetic  38.9 us (13%)
  matrix products  36.4 us (12%)
  starting transfers between devices  16.3 us (5%)
  between operations  14 us (5%)
  blocking collectives  5.85 us (2%)
    reduce_scatter x1, waiting for transfers between devices, per_device(): lax.psum_scatter(grads, 'dom', scatter_dimension=1, tiled=True)  67.3 us
    all_gather x1, waiting for transfers between devices, per_device(): lax.all_gather(master.astype(jnp.bfloat16), ('dom', 'grp'), axis=1, tiled...  27.3 us
    scatter-add x8, other arithmetic, per_device(): spreads = spreads.at[tile_src[:, column]].add(product)  27.1 us
    reduce_scatter x1, waiting for transfers between devices, per_device(): lax.psum_scatter(partial_sum.astype(jnp.bfloat16), 'grp', scatter_dimensi...  20 us
    dot_general x8, local copies, waits for them, and re-layouts, per_device(): jnp.einsum('rij,rif->rjf', tile_val[:, column], up_blocks, preferred_elem...  19.6 us
    dot_general x8, matrix products, per_device(): jnp.einsum('rij,rif->rjf', tile_val[:, column], up_blocks, preferred_elem...  14.7 us
    all_gather x1, waiting for transfers between devices, per_device(): weights_next = lax.all_gather(group_part, 'dom', axis=1, tiled=True)  13.6 us
    gather x2, local copies, waits for them, and re-layouts, aggregate(): picked = lookup[tile_src]  12.5 us
  transfers between devices with their start and end apart: 7, of which 7 were waited for; matrix products, arithmetic and copies ran while one was open for 9% of the time, Pallas kernels for 0%

commit v1 on v0

--- a/solution.py
+++ b/solution.py
@@ -106,7 +106,9 @@
     master_next = master - learn_rate * update
     rounded = master_next.astype(jnp.bfloat16)
     group_part = lax.all_gather(rounded, "grp", axis=1, tiled=True)
-    weights_next = lax.all_gather(group_part, "dom", axis=1, tiled=True)
+    weights_next = jnp.concatenate(
+        lax.all_to_all(jnp.stack([group_part] * lax.axis_size("dom")), "dom", 0, 0), axis=1
+    )
     return (layer_out, fresh_features, fresh_grads, master_next, weights_next)
 
 

time: 303 us -> 292 us (0.964)
  waiting for transfers between devices: 144 us -> 131 us
  starting transfers between devices: 16.3 us -> 20 us
    all_to_all x0 -> x1, waiting for transfers between devices: none -> 23.6 us  [per_device(): lax.all_to_all(jnp.stack([group_part] * lax.axis_size('dom')), 'dom', 0, 0)]
    reduce_scatter x1, waiting for transfers between devices: 20 us -> 4.95 us  [per_device(): lax.psum_scatter(partial_sum.astype(jnp.bfloat16), 'grp', scatter_dimensi...]
    all_gather x1 -> x0, waiting for transfers between devices: 13.6 us -> none  [per_device(): weights_next = lax.all_gather(group_part, 'dom', axis=1, tiled=True)]
    all_to_all x0 -> x1, starting transfers between devices: none -> 5.54 us  [per_device(): lax.all_to_all(jnp.stack([group_part] * lax.axis_size('dom')), 'dom', 0, 0)]
    all_to_all x1, waiting for transfers between devices: 4.25 us -> 0.01 us  [per_device(): lax.all_to_all(rim_part, 'dom', split_axis=0, concat_axis=0, tiled=True)]
    unnamed x35 -> x32, local copies, waits for them, and re-layouts: 6.47 us -> 4.2 us
  transfers between devices with their start and end apart: 7 -> 7, of which waited for: 7 -> 6; matrix products, arithmetic and copies ran while one was open for 9% -> 10% of each run, Pallas kernels for 0% -> 0%
where the time goes in v1:
time: 292 us; the launch traced here: 291 us
  waiting for transfers between devices  131 us (45%)
  local copies, waits for them, and re-layouts  45.8 us (16%)
  other arithmetic  39 us (13%)
  matrix products  36.1 us (12%)
  starting transfers between devices  20 us (7%)
  between operations  14 us (5%)
  blocking collectives  5.4 us (2%)
    reduce_scatter x1, waiting for transfers between devices, per_device(): lax.psum_scatter(grads, 'dom', scatter_dimension=1, tiled=True)  65.5 us
    all_gather x1, waiting for transfers between devices, per_device(): lax.all_gather(master.astype(jnp.bfloat16), ('dom', 'grp'), axis=1, tiled...  27.3 us
    scatter-add x8, other arithmetic, per_device(): spreads = spreads.at[tile_src[:, column]].add(product)  27.1 us
    all_to_all x1, waiting for transfers between devices, per_device(): lax.all_to_all(jnp.stack([group_part] * lax.axis_size('dom')), 'dom', 0, 0)  23.6 us
    dot_general x8, local copies, waits for them, and re-layouts, per_device(): jnp.einsum('rij,rif->rjf', tile_val[:, column], up_blocks, preferred_elem...  19.6 us
    dot_general x8, matrix products, per_device(): jnp.einsum('rij,rif->rjf', tile_val[:, column], up_blocks, preferred_elem...  14.7 us
    gather x2, local copies, waits for them, and re-layouts, aggregate(): picked = lookup[tile_src]  12.5 us
    dot_general x2, matrix products, aggregate(): jnp.einsum('rtij,rtjf->rif', tile_val, picked, preferred_element_type=jnp...  11.5 us
  transfers between devices with their start and end apart: 7, of which 6 were waited for; matrix products, arithmetic and copies ran while one was open for 10% of the time, Pallas kernels for 0%

profile of v1, /device:TPU:0, one launch (start us, length us, event | category | flops | bytes accessed | tf_op | source)
XLA Modules:
  0.0 291.2 jit_solution(2664139439705911299)
XLA Ops:
  12.7 7.3 %all-to-all-start = ((bf16[8,16,512]{2,1,0:T(8,128)(2,1)}), bf16[8,16,512]{2,1,0:T(8,128)(2,1)S(1)}, u32[]{:S(2)}, u32[]{:S(2)}) async-start(bf16[8,16,512]{2,1,0:T(8,128)(2,1)} %broadcast_select_fusion.1), calls=%async_computation | async-start | bytes 262144 | tf_op jit(solution)/shard_map/all_to_all | solution.py:48
  21.6 2.6 copy.92
  24.5 2.8 all-to-all-done
  28.6 5.7 %gather_fusion = bf16[64,128,512]{2,1,0:T(8,128)(2,1)} fusion(bf16[9,128,512]{2,1,0:T(8,128)(2,1)S(1)} %bitcast.132, s32[1024]{0:T(1024)S(1)} %pad_clamp_fusion), kind=kCustom, calls=%fused_computation.2 | custom fusion | bytes 16777472 | tf_op jit(solution)/shard_map/gather | solution.py:16
  34.3 6.3 %bitcast_convert_fusion.1 = bf16[8,512,128]{1,2,0:T(8,128)(2,1)} fusion(bf16[8,8,128,128]{3,2,1,0:T(8,128)(2,1)} %param.14, bf16[8,8,128,512]{3,2,1,0:T(8,128)(2,1)} %bitcast.143), kind=kOutput, calls=%fused_computation.18 | convolution fusion | flops 1074266112 | bytes 11534336 | tf_op jit(solution)/shard_map/rtij,rtjf->rif/dot_general | solution.py:17
  40.6 27.3 %all-gather.2.cloned.1.call-done = bf16[2,512,512]{2,1,0:T(8,128)(2,1)} async-done(((bf16[2,16,512]{2,1,0:T(8,128)(2,1)}), bf16[2,512,512]{2,1,0:T(8,128)(2,1)}) %all-gather.2.cloned.1.call-update) | async-done | bytes 1048592 | tf_op jit(solution)/shard_map/all_gather | solution.py:41
  73.4 1.9 convolution_bitcast_fusion.5
  77.0 1.9 convolution_bitcast_fusion.3
  84.4 3.1 %copy.69 = f32[8,128,512]{2,1,0:T(8,128)} copy(f32[8,128,512]{1,2,0:T(8,128)} %convolution_bitcast_fusion.7) | data formatting | bytes 4194304 | tf_op jit(solution)/shard_map/rij,rif->rjf/dot_general | solution.py:66
  89.3 3.0 %copy.75 = f32[8,128,512]{2,1,0:T(8,128)} copy(f32[8,128,512]{1,2,0:T(8,128)} %convolution_bitcast_fusion.5) | data formatting | bytes 4194304 | tf_op jit(solution)/shard_map/rij,rif->rjf/dot_general | solution.py:66
  92.4 1.9 copy.78
  94.3 3.0 %copy.81 = f32[8,128,512]{2,1,0:T(8,128)} copy(f32[8,128,512]{1,2,0:T(8,128)} %convolution_bitcast_fusion.3) | data formatting | bytes 4194304 | tf_op jit(solution)/shard_map/rij,rif->rjf/dot_general | solution.py:66
  99.2 3.1 %copy.87 = f32[8,128,512]{2,1,0:T(8,128)} copy(f32[8,128,512]{1,2,0:T(8,128)} %convolution_bitcast_fusion.1) | data formatting | bytes 4194304 | tf_op jit(solution)/shard_map/rij,rif->rjf/dot_general | solution.py:66
  104.3 3.4 %scatter_fusion = f32[9,128,512]{2,1,0:T(8,128)S(1)} fusion(f32[9,128,512]{2,1,0:T(8,128)S(1)} %broadcast_in_dim.14, s32[8]{0:T(128)S(1)} %get-tuple-element.10, f32[8,128,512]{2,1,0:T(8,128)} %copy.69), kind=kCustom, calls=%fused_computation.4 | custom fusion | flops 524288 | bytes 6291488 | tf_op jit(solution)/shard_map/scatter-add | solution.py:69
  107.7 3.3 %scatter_fusion.1 = f32[9,128,512]{2,1,0:T(8,128)S(1)} fusion(f32[9,128,512]{2,1,0:T(8,128)S(1)} %scatter_fusion, s32[8]{0:T(128)S(1)} %get-tuple-element.9, f32[8,128,512]{2,1,0:T(8,128)} %copy.72), kind=kCustom, calls=%fused_computation.5 | custom fusion | flops 524288 | bytes 6291488 | tf_op jit(solution)/shard_map/scatter-add | solution.py:69
  111.1 3.6 %scatter_fusion.2 = f32[9,128,512]{2,1,0:T(8,128)S(1)} fusion(f32[9,128,512]{2,1,0:T(8,128)S(1)} %scatter_fusion.1, s32[8]{0:T(128)S(1)} %get-tuple-element.8, f32[8,128,512]{2,1,0:T(8,128)} %copy.75), kind=kCustom, calls=%fused_computation.6 | custom fusion | flops 524288 | bytes 6291488 | tf_op jit(solution)/shard_map/scatter-add | solution.py:69
  114.6 3.4 %scatter_fusion.3 = f32[9,128,512]{2,1,0:T(8,128)S(1)} fusion(f32[9,128,512]{2,1,0:T(8,128)S(1)} %scatter_fusion.2, s32[8]{0:T(128)S(1)} %get-tuple-element.7, f32[8,128,512]{2,1,0:T(8,128)} %copy.78), kind=kCustom, calls=%fused_computation.7 | custom fusion | flops 524288 | bytes 6291488 | tf_op jit(solution)/shard_map/scatter-add | solution.py:69
  118.0 3.4 %scatter_fusion.4 = f32[9,128,512]{2,1,0:T(8,128)S(1)} fusion(f32[9,128,512]{2,1,0:T(8,128)S(1)} %scatter_fusion.3, s32[8]{0:T(128)S(1)} %get-tuple-element.11, f32[8,128,512]{2,1,0:T(8,128)} %copy.81), kind=kCustom, calls=%fused_computation.8 | custom fusion | flops 524288 | bytes 6291488 | tf_op jit(solution)/shard_map/scatter-add | solution.py:69
  121.4 3.4 %scatter_fusion.5 = f32[9,128,512]{2,1,0:T(8,128)S(1)} fusion(f32[9,128,512]{2,1,0:T(8,128)S(1)} %scatter_fusion.4, s32[8]{0:T(128)S(1)} %get-tuple-element.12, f32[8,128,512]{2,1,0:T(8,128)} %copy.84), kind=kCustom, calls=%fused_computation.9 | custom fusion | flops 524288 | bytes 6291488 | tf_op jit(solution)/shard_map/scatter-add | solution.py:69
  124.7 3.4 %scatter_fusion.6 = f32[9,128,512]{2,1,0:T(8,128)S(1)} fusion(f32[9,128,512]{2,1,0:T(8,128)S(1)} %scatter_fusion.5, s32[8]{0:T(128)S(1)} %get-tuple-element.13, f32[8,128,512]{2,1,0:T(8,128)} %copy.87), kind=kCustom, calls=%fused_computation.10 | custom fusion | flops 524288 | bytes 6291488 | tf_op jit(solution)/shard_map/scatter-add | solution.py:69
  128.1 3.4 %scatter_fusion.7 = f32[9,128,512]{2,1,0:T(8,128)S(1)} fusion(f32[9,128,512]{2,1,0:T(8,128)S(1)} %scatter_fusion.6, s32[8]{0:T(128)S(1)} %get-tuple-element.6, f32[8,128,512]{2,1,0:T(8,128)} %copy.90), kind=kCustom, calls=%fused_computation.11 | custom fusion | flops 524288 | bytes 6291488 | tf_op jit(solution)/shard_map/scatter-add | solution.py:69
  138.0 6.8 %gather_fusion.1 = bf16[64,128,512]{2,1,0:T(8,128)(2,1)} fusion(bf16[9,128,512]{2,1,0:T(8,128)(2,1)} %bitcast.133, s32[1024]{0:T(1024)S(1)} %pad_clamp_fusion), kind=kCustom, calls=%fused_computation.3 | custom fusion | bytes 16777472 | tf_op jit(solution)/shard_map/gather | solution.py:16
  144.8 5.3 %bitcast_convert_fusion = bf16[8,512,128]{1,2,0:T(8,128)(2,1)S(1)} fusion(bf16[8,8,128,128]{3,2,1,0:T(8,128)(2,1)} %param.14, bf16[8,8,128,512]{3,2,1,0:T(8,128)(2,1)} %bitcast.142), kind=kOutput, calls=%fused_computation.17 | convolution fusion | flops 1074266112 | bytes 11534336 | tf_op jit(solution)/shard_map/rtij,rtjf->rif/dot_general | solution.py:17
  155.1 65.5 %reduce-scatter.3.cloned.1.call-done = f32[2,64,512]{2,1,0:T(8,128)} async-done(((f32[2,512,512]{2,1,0:T(8,128)}), f32[2,64,512]{2,1,0:T(8,128)}) %reduce-scatter.3.cloned.1.call-update) | async-done | bytes 262160 | tf_op jit(solution)/shard_map/reduce_scatter | solution.py:92
  223.0 3.6 %all-to-all-start.1 = ((bf16[8,16,512]{2,1,0:T(8,128)(2,1)}), bf16[8,16,512]{2,1,0:T(8,128)(2,1)S(1)}, u32[]{:S(2)}, u32[]{:S(2)}) async-start(bf16[8,16,512]{2,1,0:T(8,128)(2,1)} %broadcast_select_fusion), calls=%async_computation.1 | async-start | bytes 262144 | tf_op jit(solution)/shard_map/all_to_all | solution.py:73
  227.3 6.7 %all-to-all-done.1 = bf16[8,16,512]{2,1,0:T(8,128)(2,1)S(1)} async-done(((bf16[8,16,512]{2,1,0:T(8,128)(2,1)}), bf16[8,16,512]{2,1,0:T(8,128)(2,1)S(1)}, u32[]{:S(2)}, u32[]{:S(2)}) %all-to-all-start.1) | async-done | bytes 131104 | tf_op jit(solution)/shard_map/all_to_all | solution.py:73
  234.0 3.4 %all-to-all-start.2 = ((bf16[8,16,512]{2,1,0:T(8,128)(2,1)}), bf16[8,16,512]{2,1,0:T(8,128)(2,1)S(1)}, u32[]{:S(2)}, u32[]{:S(2)}) async-start(bf16[8,16,512]{2,1,0:T(8,128)(2,1)} %bitcast.154), calls=%async_computation.2 | async-start | bytes 262144 | tf_op jit(solution)/shard_map/all_to_all | solution.py:76
  237.4 5.0 %reduce-scatter.5.cloned.1.call-done = bf16[2,16,512]{2,1,0:T(8,128)(2,1)} async-done(((bf16[2,64,512]{2,1,0:T(8,128)(2,1)}), bf16[2,16,512]{2,1,0:T(8,128)(2,1)}) %reduce-scatter.5.cloned.1.call-update) | async-done | bytes 32784 | tf_op jit(solution)/shard_map/reduce_scatter | solution.py:94
  243.9 5.4 %all_gather.7 = bf16[2,64,512]{2,1,0:T(8,128)(2,1)S(1)} all-gather(bf16[2,16,512]{2,1,0:T(8,128)(2,1)S(1)} %get-tuple-element.14), channel_id=1, replica_groups=mesh['dom'=8,'grp'=4] {'grp'}, dimensions={1}, use_global_device_ids=true | all-gather | bytes 163840 | tf_op jit(solution)/shard_map/all_gather | solution.py:108
  250.4 5.5 %all-to-all-start.3 = ((bf16[8,2,64,512]{3,2,1,0:T(8,128)(2,1)}), bf16[8,2,64,512]{3,2,1,0:T(8,128)(2,1)S(1)}, u32[]{:S(2)}, u32[]{:S(2)}) async-start(bf16[8,2,64,512]{3,2,1,0:T(8,128)(2,1)} %stack.11), calls=%async_computation.5 | async-start | bytes 2097152 | tf_op jit(solution)/shard_map/all_to_all | solution.py:110
  256.0 2.7 convolution_convert_fusion.1
  258.7 23.6 %all-to-all-done.3 = bf16[8,2,64,512]{3,2,1,0:T(8,128)(2,1)S(1)} async-done(((bf16[8,2,64,512]{3,2,1,0:T(8,128)(2,1)}), bf16[8,2,64,512]{3,2,1,0:T(8,128)(2,1)S(1)}, u32[]{:S(2)}, u32[]{:S(2)}) %all-to-all-start.3) | async-done | bytes 1048608 | tf_op jit(solution)/shard_map/all_to_all | solution.py:110
  (75 shorter events, 46.8 us)
Async XLA Ops:
  7.2 60.7 %copy-start = (bf16[1024,512]{1,0:T(8,128)(2,1)S(1)}, bf16[1024,512]{1,0:T(8,128)(2,1)}, u32[]{:S(2)}) copy-start(bf16[1024,512]{1,0:T(8,128)(2,1)} %param.18) | copy-start | bytes 3145732
  7.2 14.3 %copy-start.12 = (s32[8,8]{1,0:T(8,128)S(1)}, s32[8,8]{1,0:T(8,128)}, u32[]{:S(2)}) copy-start(s32[8,8]{1,0:T(8,128)} %param.13) | copy-start | bytes 772
  7.2 60.7 %all-gather.2.cloned.1.call-start = ((), (), s32[]{:S(2)}) async-start(), calls=%async_computation.6 | async-start | bytes 1081344 | tf_op jit(solution)/shard_map/all_gather | solution.py:41
  12.7 14.6 %all-to-all-start = ((bf16[8,16,512]{2,1,0:T(8,128)(2,1)}), bf16[8,16,512]{2,1,0:T(8,128)(2,1)S(1)}, u32[]{:S(2)}, u32[]{:S(2)}) async-start(bf16[8,16,512]{2,1,0:T(8,128)(2,1)} %broadcast_select_fusion.1), calls=%async_computation | async-start | bytes 262144 | tf_op jit(solution)/shard_map/all_to_all | solution.py:48
  19.9 200.7 %reduce-scatter.3.cloned.1.call-start = ((), (), s32[]{:S(2)}) async-start(), calls=%async_computation.7 | async-start | bytes 2359296 | tf_op jit(solution)/shard_map/reduce_scatter | solution.py:92
  40.6 29.1 %copy-start.1 = (bf16[8,8,128,128]{3,2,1,0:T(8,128)(2,1)S(1)}, bf16[8,8,128,128]{3,2,1,0:T(8,128)(2,1)}, u32[]{:S(2)}) copy-start(bf16[8,8,128,128]{3,2,1,0:T(8,128)(2,1)} %param.14) | copy-start | bytes 6291460
  84.4 3.1 %copy-start.5 = (f32[8,128,512]{1,2,0:T(8,128)S(1)}, f32[8,128,512]{1,2,0:T(8,128)}, u32[]{:S(2)}) copy-start(f32[8,128,512]{1,2,0:T(8,128)} %convolution_bitcast_fusion.6) | copy-start | bytes 6291460
  89.3 3.0 %copy-start.4 = (f32[8,128,512]{1,2,0:T(8,128)S(1)}, f32[8,128,512]{1,2,0:T(8,128)}, u32[]{:S(2)}) copy-start(f32[8,128,512]{1,2,0:T(8,128)} %convolution_bitcast_fusion.4) | copy-start | bytes 6291460
  94.3 3.0 %copy-start.3 = (f32[8,128,512]{1,2,0:T(8,128)S(1)}, f32[8,128,512]{1,2,0:T(8,128)}, u32[]{:S(2)}) copy-start(f32[8,128,512]{1,2,0:T(8,128)} %convolution_bitcast_fusion.2) | copy-start | bytes 6291460
  99.1 3.1 %copy-start.2 = (f32[8,128,512]{1,2,0:T(8,128)S(1)}, f32[8,128,512]{1,2,0:T(8,128)}, u32[]{:S(2)}) copy-start(f32[8,128,512]{1,2,0:T(8,128)} %convolution_bitcast_fusion) | copy-start | bytes 6291460
  131.5 1.6 copy-start.6
  131.5 1.8 copy-start.11
  131.5 2.2 copy-start.14
  135.1 1.7 copy-start.7
  135.1 1.7 copy-start.13
  150.1 1.0 copy-start.9
  150.1 1.6 copy-start.8
  153.3 89.1 %reduce-scatter.5.cloned.1.call-start = ((), (), s32[]{:S(2)}) async-start(), calls=%async_computation.8 | async-start | bytes 163840 | tf_op jit(solution)/shard_map/reduce_scatter | solution.py:94
  223.0 11.0 %all-to-all-start.1 = ((bf16[8,16,512]{2,1,0:T(8,128)(2,1)}), bf16[8,16,512]{2,1,0:T(8,128)(2,1)S(1)}, u32[]{:S(2)}, u32[]{:S(2)}) async-start(bf16[8,16,512]{2,1,0:T(8,128)(2,1)} %broadcast_select_fusion), calls=%async_computation.1 | async-start | bytes 262144 | tf_op jit(solution)/shard_map/all_to_all | solution.py:73
  227.3 28.7 %copy-start.10 = (bf16[8,512,128]{1,2,0:T(8,128)(2,1)S(1)}, bf16[8,512,128]{1,2,0:T(8,128)(2,1)}, u32[]{:S(2)}) copy-start(bf16[8,512,128]{1,2,0:T(8,128)(2,1)} %copy-done.9) | copy-start | bytes 3145732
  234.0 15.4 %all-to-all-start.2 = ((bf16[8,16,512]{2,1,0:T(8,128)(2,1)}), bf16[8,16,512]{2,1,0:T(8,128)(2,1)S(1)}, u32[]{:S(2)}, u32[]{:S(2)}) async-start(bf16[8,16,512]{2,1,0:T(8,128)(2,1)} %bitcast.154), calls=%async_computation.2 | async-start | bytes 262144 | tf_op jit(solution)/shard_map/all_to_all | solution.py:76
  250.4 31.8 %all-to-all-start.3 = ((bf16[8,2,64,512]{3,2,1,0:T(8,128)(2,1)}), bf16[8,2,64,512]{3,2,1,0:T(8,128)(2,1)S(1)}, u32[]{:S(2)}, u32[]{:S(2)}) async-start(bf16[8,2,64,512]{3,2,1,0:T(8,128)(2,1)} %stack.11), calls=%async_computation.5 | async-start | bytes 2097152 | tf_op jit(solution)/shard_map/all_to_all | solution.py:110
Sparse Core Ops, SparseCore 0:
  11.5 56.3 all-gather.1
  153.4 67.1 reduce-scatter.2
  223.6 18.6 reduce-scatter.4
